TPU v7x, 32 devices: a whole 2x2x4 slice. The times are simulated.
32 devices in a mesh: wide: 16 (over z, x, core), head: 2 (over y).
Axes of the slice: x: 2, y: 2, z: 4, core: 2. Of those that a mesh axis runs over, the one named last changes fastest.
Arguments:
- queries: bfloat16 [8192, 8192], P(('wide', 'head')), may hold values from -6 to 6
- keys: bfloat16 [8192, 1024], P(('wide', 'head')), may hold values from -6 to 6
- values: bfloat16 [8192, 1024], P(('wide', 'head')), may hold values from -6 to 6
- out_rows: bfloat16 [8192, 8192], P(('wide', 'head')), may hold values from -3 to 3
- output_gradient: bfloat16 [8192, 8192], P(('wide', 'head')), may hold values from -3 to 3
- log_norm_rows: float32 [8192, 64], P(('wide', 'head')), may hold values from 4 to 8
- doc_lengths: int32 [16], replicated, may hold values from 1 to 768, 8192 in all
Outputs:
- q_grad: float32 [8192, 8192], P(('wide', 'head'))
- key_gradient: float32 [8192, 1024], P(('wide', 'head'))
- value_gradient: float32 [8192, 1024], P(('wide', 'head'))
Inputs may be any that keep to these rules, and one draw needn't show every extreme that they name: `doc_lengths`: 16 document lengths in order; they sum to 8192.
All inputs are finite; a program needn't handle non-finite values.
Results may differ from a plain program's by a relative error of at most 0.0058.
Values may be sent and summed in bfloat16 or wider, within the bound.
A program may use at most 192 MiB of HBM per device.

v0:
```python
import functools
import math

import jax
import jax.numpy as jnp
from jax import lax
from jax.experimental import pallas as pl
from jax.experimental.pallas import tpu as pltpu
from jax.sharding import PartitionSpec as P

AXES = ("wide", "head")
LOG2E = math.log2(math.e)


MESH = pl.DeviceIdType.MESH


def attention_kernel(reach, lanes, tile, scaling, sizes, *refs):
    pieces = reach.bit_length()
    q_ref, g_ref, o_ref, k_hbm, v_hbm, norm_ref, start_ref, dq_ref, dk_ref, dv_ref = refs[:10]
    kv, sent, landed, dk_win, dv_win, q_all, g_all, dq_acc, norm_all, delta_all, bias = refs[10:21]
    load_sem, in_send, in_recv, out_send, out_recv = refs[21:]
    rows = k_hbm.shape[0]
    groups = norm_ref.shape[0]
    size = q_ref.shape[1] // groups
    heads = k_hbm.shape[1] // size
    halves = rows // lanes
    own = reach * rows
    length = own + lanes
    full = length // tile
    rest = length - full * tile
    nt = (((1,), (1,)), ((), ()))
    head = pl.program_id(0)
    shards = sizes[0] * sizes[1]
    shard = lax.axis_index(AXES[0]) * sizes[1] + lax.axis_index(AXES[1])

    def device(by):
        other = lax.rem(shard + by + shards, shards)
        return (other // sizes[1], lax.rem(other, sizes[1]))

    def cut_of(c):
        return pl.ds(pl.multiple_of(c * size, size), size)

    def gather(d, c):
        n = rows << d
        at = own + rows - n
        return pltpu.make_async_remote_copy(
            src_ref=kv.at[:, pl.ds(at, n), cut_of(c)],
            dst_ref=kv.at[:, pl.ds(at - n, n), cut_of(c)],
            send_sem=in_send.at[d, c],
            recv_sem=in_recv.at[d, c],
            device_id=device(1 << d),
            device_id_type=MESH,
        )

    def back(d, c):
        n = rows << d
        at = own + rows - 2 * n
        return pltpu.make_async_remote_copy(
            src_ref=sent.at[:, pl.ds(at, n), cut_of(c)],
            dst_ref=landed.at[:, pl.ds(at, n), cut_of(c)],
            send_sem=out_send.at[d, c],
            recv_sem=out_recv.at[d, c],
            device_id=device(-(1 << d)),
            device_id_type=MESH,
        )

    def forward(d, c):
        gather(d - 1, c).wait_recv()
        gather(d, c).start()

    def collect(d, c):
        n = rows << d
        at = own + rows - 2 * n
        back(d, c).wait_recv()
        cut = cut_of(c)
        if n > rows:
            near = pl.ds(own + rows - n, n - rows)
            got = landed[:, pl.ds(at, n - rows), cut].astype(jnp.float32)
            sent[:, near, cut] = (sent[:, near, cut].astype(jnp.float32) + got).astype(jnp.bfloat16)
        last = landed[:, pl.ds(at + n - rows, rows), cut].astype(jnp.float32)
        dk_ref[:, cut] += last[0]
        dv_ref[:, cut] += last[1]
        if d > 0:
            back(d - 1, c).start()

    @pl.when(head == 0)
    def _():
        barrier = pltpu.get_barrier_semaphore()
        for d in range(pieces):
            for by in (1 << d, -(1 << d)):
                pl.semaphore_signal(barrier, inc=1, device_id=device(by), device_id_type=MESH)
        loads = [
            pltpu.make_async_copy(ref, kv.at[n, pl.ds(own, rows)], load_sem.at[n])
            for n, ref in enumerate((k_hbm, v_hbm))
        ]
        for load in loads:
            load.start()
        for load in loads:
            load.wait()
        pl.semaphore_wait(barrier, 2 * pieces)
        for c in range(heads):
            gather(0, c).start()
        for half in range(halves):
            end = own + (half + 1) * lanes
            for i in range(bias.shape[1]):
                key_at = lax.broadcasted_iota(jnp.int32, (tile, lanes), 0) + (end - (i + 1) * tile)
                query_at = lax.broadcasted_iota(jnp.int32, (tile, lanes), 1) + (end - lanes)
                start = start_ref[:, half * lanes : (half + 1) * lanes]
                allowed = (key_at >= start) & (key_at <= query_at)
                bias[half, i] = jnp.where(allowed, 0.0, -1e30)
        for d in range(1, pieces):
            for c in range(min(pieces - d, heads)):
                forward(d, c)

    for d in range(1, pieces):
        ahead = head + pieces - d

        @pl.when(ahead < heads)
        def _():
            forward(d, ahead)

    dk_win[...] = jnp.zeros_like(dk_win)
    dv_win[...] = jnp.zeros_like(dv_win)
    dq_acc[...] = jnp.zeros_like(dq_acc)
    for a in range(groups):
        cut = slice(a * size, (a + 1) * size)
        product = g_ref[:, cut].astype(jnp.float32) * o_ref[:, cut].astype(jnp.float32)
        delta = jnp.sum(product.T, axis=0, keepdims=True)
        for half in range(halves):
            to = slice(a * lanes, (a + 1) * lanes)
            here = slice(half * lanes, (half + 1) * lanes)
            q_all[half, to] = q_ref[here, cut]
            g_all[half, to] = g_ref[here, cut]
            norm_all[half, :, to] = norm_ref[a : a + 1, here]
            delta_all[half, :, to] = delta[:, here]
    span = 2 * lanes if groups % 2 == 0 else lanes
    gather(pieces - 1, head).wait_recv()
    mine = cut_of(head)

    for half in range(halves):
        end = own + (half + 1) * lanes

        def terms(first, count, i):
            at = pl.ds(first, count)
            k_tile = kv[0, at, mine]
            v_tile = kv[1, at, mine]
            masked = bias[half, i][tile - count :]
            masked = jnp.concatenate([masked] * (span // lanes), axis=1)
            lows = []
            for part in range(groups * lanes // span):
                cut = slice(part * span, (part + 1) * span)
                s = lax.dot_general(k_tile, q_all[half, cut], nt, preferred_element_type=jnp.float32)
                p = jnp.exp2(s * (scaling * LOG2E) - norm_all[half, :, cut] + masked)
                dp = lax.dot_general(v_tile, g_all[half, cut], nt, preferred_element_type=jnp.float32)
                ds = (p * (dp - delta_all[half, :, cut])).astype(jnp.bfloat16)
                lows.append((p.astype(jnp.bfloat16), ds))
            p_low = jnp.concatenate([low[0] for low in lows], axis=1)
            ds_low = jnp.concatenate([low[1] for low in lows], axis=1)
            dv_win[at, :] += jnp.dot(p_low, g_all[half], preferred_element_type=jnp.float32)
            dk_win[at, :] += jnp.dot(ds_low, q_all[half], preferred_element_type=jnp.float32)
            dq_acc[half] += jnp.dot(k_tile.T, ds_low, preferred_element_type=jnp.float32)

        def step(i, carry):
            terms(pl.multiple_of(end - (i + 1) * tile, lanes), tile, i)
            return carry

        lax.fori_loop(0, full, step, 0)
        if rest:
            terms(end - length, rest, full)
    dk_ref[:, mine] = dk_win[own:] * scaling
    dv_ref[:, mine] = dv_win[own:]
    sent[0, pl.ds(0, own), mine] = (dk_win[:own] * scaling).astype(jnp.bfloat16)
    sent[1, pl.ds(0, own), mine] = dv_win[:own].astype(jnp.bfloat16)
    for half in range(halves):
        for a in range(groups):
            here = slice(half * lanes, (half + 1) * lanes)
            turn = dq_acc[half, :, a * lanes : (a + 1) * lanes].T
            dq_ref[here, a * size : (a + 1) * size] = turn * scaling
    back(pieces - 1, head).start()
    for d in range(pieces):
        behind = head - (pieces - d)

        @pl.when(behind >= 0)
        def _():
            collect(d, behind)

    @pl.when(head == heads - 1)
    def _():
        for late in range(1, pieces + 1):
            for d in range(pieces):
                c = heads - 1 + late - (pieces - d)
                if 0 <= c < heads:
                    collect(d, c)
        for d in range(pieces):
            for c in range(heads):
                gather(d, c).wait_send()
                back(d, c).wait_send()


def attention(q, g, o, k, v, norm, start, sizes, reach):
    rows, width = q.shape
    pieces = reach.bit_length()
    groups = width // k.shape[1]
    heads = norm.shape[0] // groups
    size = k.shape[1] // heads
    lanes = min(128, rows)
    tile = 2 * lanes
    halves = rows // lanes
    window = (reach + 1) * rows
    wide = pl.BlockSpec((rows, groups * size), lambda h: (0, h))
    whole = pl.BlockSpec(k.shape, lambda h: (0, 0))
    here = pl.BlockSpec(memory_space=pl.ANY)
    copies = pltpu.SemaphoreType.DMA((pieces, heads))
    return pl.pallas_call(
        functools.partial(attention_kernel, reach, lanes, tile, 1.0 / math.sqrt(size), sizes),
        grid=(heads,),
        in_specs=[
            wide,
            wide,
            wide,
            here,
            here,
            pl.BlockSpec((groups, rows), lambda h: (h, 0)),
            pl.BlockSpec((1, rows), lambda h: (0, 0)),
        ],
        out_specs=[wide, whole, whole],
        scratch_shapes=[
            pltpu.VMEM((2, window, k.shape[1]), jnp.bfloat16),
            pltpu.VMEM((2, reach * rows, k.shape[1]), jnp.bfloat16),
            pltpu.VMEM((2, reach * rows, k.shape[1]), jnp.bfloat16),
            pltpu.VMEM((window, size), jnp.float32),
            pltpu.VMEM((window, size), jnp.float32),
            pltpu.VMEM((halves, groups * lanes, size), jnp.bfloat16),
            pltpu.VMEM((halves, groups * lanes, size), jnp.bfloat16),
            pltpu.VMEM((halves, size, groups * lanes), jnp.float32),
            pltpu.VMEM((halves, 1, groups * lanes), jnp.float32),
            pltpu.VMEM((halves, 1, groups * lanes), jnp.float32),
            pltpu.VMEM((halves, pl.cdiv(reach * rows + lanes, tile), tile, lanes), jnp.float32),
            pltpu.SemaphoreType.DMA((2,)),
            copies,
            copies,
            copies,
            copies,
        ],
        out_shape=[
            jax.ShapeDtypeStruct((rows, width), jnp.float32),
            jax.ShapeDtypeStruct(k.shape, jnp.float32),
            jax.ShapeDtypeStruct(k.shape, jnp.float32),
        ],
        compiler_params=pltpu.CompilerParams(
            dimension_semantics=("arbitrary",),
            vmem_limit_bytes=56 << 20,
            collective_id=0,
            has_side_effects=True,
        ),
    )(q, g, o, k, v, norm, start)


def on_device(sizes, queries, keys, values, out_rows, output_gradient, log_norm_rows, doc_lengths):
    rows = queries.shape[0]
    shards = sizes[0] * sizes[1]
    reach = shards // 8 - 1
    shard = lax.axis_index(AXES)
    starts = jnp.cumsum(doc_lengths) - doc_lengths
    position = shard * rows + jnp.arange(rows, dtype=jnp.int32)
    start = jnp.max(
        jnp.where(starts[None, :] <= position[:, None], starts[None, :], 0), axis=1
    )
    start = (start - (shard - reach) * rows).astype(jnp.int32).reshape(1, rows)
    norm = (log_norm_rows * LOG2E).T
    return tuple(
        attention(
            queries, output_gradient, out_rows, keys, values, norm, start, sizes, reach
        )
    )


def solution(mesh):
    sizes = (mesh.shape["wide"], mesh.shape["head"])
    rows = P(AXES, None)
    return jax.shard_map(
        functools.partial(on_device, sizes),
        mesh=mesh,
        in_specs=(rows,) * 6 + (P(),),
        out_specs=(rows,) * 3,
        check_vma=False,
    )
```

profile of v0, /device:TPU:1, one launch (start us, length us, event | category | flops | bytes accessed | tf_op | source)
XLA Modules:
  0.0 112.3 jit_solution(5892336746595031916)
XLA Ops:
  0.6 0.7 copy.12
  1.4 0.1 reduce
  1.5 0.7 sub.22
  2.2 0.1 select_reduce_fusion
  2.3 0.6 broadcast_subtract_fusion
  2.9 1.5 %multiply_bitcast_fusion.refs_5_ = f32[64,256]{1,0:T(8,128)} fusion(f32[256,64]{0,1:T(8,128)} %param.12), kind=kLoop, calls=%fused_computation | loop fusion | flops 16384 | bytes 131072 | tf_op jit(solution)/shard_map/transpose | solution.py:271
  4.3 98.2 %shard_map.94 = (f32[256,8192]{1,0:T(8,128)}, f32[256,1024]{1,0:T(8,128)}, f32[256,1024]{1,0:T(8,128)}) custom-call(bf16[256,8192]{1,0:T(8,128)(2,1)} %refs_0_.1, bf16[256,8192]{1,0:T(8,128)(2,1)} %refs_1_.1, bf16[256,8192]{1,0:T(8,128)(2,1)} %refs_2_.1, bf16[256,1024]{1,0:T(8,128)(2,1)} %refs_3_.1, bf16[256,1024]{1,0:T(8,128)(2,1)} %refs_4_.1, ...), custom_call_target="tpu_custom_call" | custom-call | tf_op jit(solution)/shard_map/pallas_call | solution.py:215
  102.5 0.0 copy-start.1
  102.5 0.0 copy-start
  102.6 7.8 %copy.16 = f32[256,8192]{1,0:T(8,128)} copy(f32[256,8192]{1,0:T(8,128)} %get-tuple-element.6) | data formatting | bytes 16777216
  110.4 0.0 copy-done.1
  110.4 1.0 copy.17
  111.4 0.0 copy-done
  111.4 1.0 copy.18
  (2 shorter events, 0.0 us)
Async XLA Ops:
  102.5 7.9 %copy-start.1 = (f32[256,1024]{1,0:T(8,128)S(1)}, f32[256,1024]{1,0:T(8,128)}, u32[]{:S(2)}) copy-start(f32[256,1024]{1,0:T(8,128)} %get-tuple-element.7) | copy-start | bytes 3145732
  102.5 8.8 %copy-start = (f32[256,1024]{1,0:T(8,128)S(1)}, f32[256,1024]{1,0:T(8,128)}, u32[]{:S(2)}) copy-start(f32[256,1024]{1,0:T(8,128)} %get-tuple-element.8) | copy-start | bytes 3145732
where the time goes:
time: 113 us; the launch traced here: 112 us
  Pallas kernels  98.2 us (87%)
  local copies, waits for them, and re-layouts  10.5 us (9%)
  other arithmetic  2.95 us (3%)
    pallas_call x1, Pallas kernels, attention(): pl.pallas_call(functools.partial(attention_kernel, reach, lanes, tile, 1....  98.2 us
    unnamed x7, local copies, waits for them, and re-layouts  9.78 us

commit v1 on v0

--- a/solution.py
+++ b/solution.py
@@ -31,6 +31,7 @@
     rest = length - full * tile
     nt = (((1,), (1,)), ((), ()))
     head = pl.program_id(0)
+    lead = pieces + 1
     shards = sizes[0] * sizes[1]
     shard = lax.axis_index(AXES[0]) * sizes[1] + lax.axis_index(AXES[1])
 
@@ -99,7 +100,7 @@
         for load in loads:
             load.wait()
         pl.semaphore_wait(barrier, 2 * pieces)
-        for c in range(heads):
+        for c in range(min(lead, heads)):
             gather(0, c).start()
         for half in range(halves):
             end = own + (half + 1) * lanes
@@ -109,17 +110,6 @@
                 start = start_ref[:, half * lanes : (half + 1) * lanes]
                 allowed = (key_at >= start) & (key_at <= query_at)
                 bias[half, i] = jnp.where(allowed, 0.0, -1e30)
-        for d in range(1, pieces):
-            for c in range(min(pieces - d, heads)):
-                forward(d, c)
-
-    for d in range(1, pieces):
-        ahead = head + pieces - d
-
-        @pl.when(ahead < heads)
-        def _():
-            forward(d, ahead)
-
     dk_win[...] = jnp.zeros_like(dk_win)
     dv_win[...] = jnp.zeros_like(dv_win)
     dq_acc[...] = jnp.zeros_like(dq_acc)
@@ -135,11 +125,17 @@
             norm_all[half, :, to] = norm_ref[a : a + 1, here]
             delta_all[half, :, to] = delta[:, here]
     span = 2 * lanes if groups % 2 == 0 else lanes
-    gather(pieces - 1, head).wait_recv()
     mine = cut_of(head)
 
-    for half in range(halves):
+    @pl.when(head == 0)
+    def _():
+        for d in range(1, pieces):
+            for c in range(min(pieces - d, heads)):
+                forward(d, c)
+
+    def tiles(half, near):
         end = own + (half + 1) * lanes
+        reached = min(full, ((half + 1) * lanes + rows) // tile)
 
         def terms(first, count, i):
             at = pl.ds(first, count)
@@ -165,9 +161,30 @@
             terms(pl.multiple_of(end - (i + 1) * tile, lanes), tile, i)
             return carry
 
-        lax.fori_loop(0, full, step, 0)
-        if rest:
-            terms(end - length, rest, full)
+        if near:
+            lax.fori_loop(0, reached, step, 0)
+        else:
+            lax.fori_loop(reached, full, step, 0)
+            if rest:
+                terms(end - length, rest, full)
+
+    for half in reversed(range(halves)):
+        tiles(half, True)
+
+    @pl.when(head + lead < heads)
+    def _():
+        gather(0, head + lead).start()
+
+    for d in range(1, pieces):
+        ahead = head + pieces - d
+
+        @pl.when(ahead < heads)
+        def _():
+            forward(d, ahead)
+
+    gather(pieces - 1, head).wait_recv()
+    for half in range(halves):
+        tiles(half, False)
     dk_ref[:, mine] = dk_win[own:] * scaling
     dv_ref[:, mine] = dv_win[own:]
     sent[0, pl.ds(0, own), mine] = (dk_win[:own] * scaling).astype(jnp.bfloat16)

time: 113 us -> 107 us (0.947)
  Pallas kernels: 98.2 us -> 92.8 us
    pallas_call x1, Pallas kernels: 98.2 us -> 92.8 us  [attention(): pl.pallas_call(functools.partial(attention_kernel, reach, lanes, tile, 1....]
where the time goes in v1:
time: 107 us
  Pallas kernels  92.8 us (87%)
  local copies, waits for them, and re-layouts  10.5 us (10%)
  other arithmetic  2.95 us (3%)
    pallas_call x1, Pallas kernels, attention(): pl.pallas_call(functools.partial(attention_kernel, reach, lanes, tile, 1....  92.8 us
    unnamed x7, local copies, waits for them, and re-layouts  9.78 us

profile of v1, /device:TPU:1, one launch (start us, length us, event | category | flops | bytes accessed | tf_op | source)
XLA Modules:
  0.0 107.0 jit_solution(13403620399771736914)
XLA Ops:
  0.6 0.7 copy.12
  1.4 0.1 reduce
  1.5 0.7 sub.22
  2.2 0.1 select_reduce_fusion
  2.3 0.6 broadcast_subtract_fusion
  2.9 1.5 %multiply_bitcast_fusion.refs_5_ = f32[64,256]{1,0:T(8,128)} fusion(f32[256,64]{0,1:T(8,128)} %param.12), kind=kLoop, calls=%fused_computation | loop fusion | flops 16384 | bytes 131072 | tf_op jit(solution)/shard_map/transpose | solution.py:288
  4.3 92.8 %shard_map.94 = (f32[256,8192]{1,0:T(8,128)}, f32[256,1024]{1,0:T(8,128)}, f32[256,1024]{1,0:T(8,128)}) custom-call(bf16[256,8192]{1,0:T(8,128)(2,1)} %refs_0_.1, bf16[256,8192]{1,0:T(8,128)(2,1)} %refs_1_.1, bf16[256,8192]{1,0:T(8,128)(2,1)} %refs_2_.1, bf16[256,1024]{1,0:T(8,128)(2,1)} %refs_3_.1, bf16[256,1024]{1,0:T(8,128)(2,1)} %refs_4_.1, ...), custom_call_target="tpu_custom_call" | custom-call | tf_op jit(solution)/shard_map/pallas_call | solution.py:232
  97.2 0.0 copy-start.1
  97.2 0.0 copy-start
  97.2 7.8 %copy.16 = f32[256,8192]{1,0:T(8,128)} copy(f32[256,8192]{1,0:T(8,128)} %get-tuple-element.6) | data formatting | bytes 16777216
  105.0 0.0 copy-done.1
  105.0 1.0 copy.17
  106.0 0.0 copy-done
  106.0 1.0 copy.18
  (2 shorter events, 0.0 us)
Async XLA Ops:
  97.2 7.9 %copy-start.1 = (f32[256,1024]{1,0:T(8,128)S(1)}, f32[256,1024]{1,0:T(8,128)}, u32[]{:S(2)}) copy-start(f32[256,1024]{1,0:T(8,128)} %get-tuple-element.7) | copy-start | bytes 3145732
  97.2 8.8 %copy-start = (f32[256,1024]{1,0:T(8,128)S(1)}, f32[256,1024]{1,0:T(8,128)}, u32[]{:S(2)}) copy-start(f32[256,1024]{1,0:T(8,128)} %get-tuple-element.8) | copy-start | bytes 3145732

commit v2 on v1

--- a/solution.py
+++ b/solution.py
@@ -168,8 +168,10 @@
             if rest:
                 terms(end - length, rest, full)
 
-    for half in reversed(range(halves)):
-        tiles(half, True)
+    @pl.when(head == 0)
+    def _():
+        for half in reversed(range(halves)):
+            tiles(half, True)
 
     @pl.when(head + lead < heads)
     def _():
@@ -185,16 +187,25 @@
     gather(pieces - 1, head).wait_recv()
     for half in range(halves):
         tiles(half, False)
+    far = own - rows
+    sent[0, pl.ds(0, far), mine] = (dk_win[:far] * scaling).astype(jnp.bfloat16)
+    sent[1, pl.ds(0, far), mine] = dv_win[:far].astype(jnp.bfloat16)
+    back(pieces - 1, head).start()
+
+    @pl.when(head > 0)
+    def _():
+        for half in range(halves):
+            tiles(half, True)
+
     dk_ref[:, mine] = dk_win[own:] * scaling
     dv_ref[:, mine] = dv_win[own:]
-    sent[0, pl.ds(0, own), mine] = (dk_win[:own] * scaling).astype(jnp.bfloat16)
-    sent[1, pl.ds(0, own), mine] = dv_win[:own].astype(jnp.bfloat16)
+    sent[0, pl.ds(far, rows), mine] = (dk_win[far:own] * scaling).astype(jnp.bfloat16)
+    sent[1, pl.ds(far, rows), mine] = dv_win[far:own].astype(jnp.bfloat16)
     for half in range(halves):
         for a in range(groups):
             here = slice(half * lanes, (half + 1) * lanes)
             turn = dq_acc[half, :, a * lanes : (a + 1) * lanes].T
-            dq_ref[here, a * size : (a + 1) * size] = turn * scaling
-    back(pieces - 1, head).start()
+            dq_ref[here, a * size : (a + 1) * size] = (turn * scaling).astype(dq_ref.dtype)
     for d in range(pieces):
         behind = head - (pieces - d)
 
@@ -261,7 +272,7 @@
             copies,
         ],
         out_shape=[
-            jax.ShapeDtypeStruct((rows, width), jnp.float32),
+            jax.ShapeDtypeStruct((rows, width), jnp.bfloat16),
             jax.ShapeDtypeStruct(k.shape, jnp.float32),
             jax.ShapeDtypeStruct(k.shape, jnp.float32),
         ],
@@ -286,11 +297,10 @@
     )
     start = (start - (shard - reach) * rows).astype(jnp.int32).reshape(1, rows)
     norm = (log_norm_rows * LOG2E).T
-    return tuple(
-        attention(
-            queries, output_gradient, out_rows, keys, values, norm, start, sizes, reach
-        )
+    dq, dk, dv = attention(
+        queries, output_gradient, out_rows, keys, values, norm, start, sizes, reach
     )
+    return (dq.astype(jnp.float32), dk, dv)
 
 
 def solution(mesh):

time: 107 us -> 98.2 us (0.918)
  Pallas kernels: 92.8 us -> 84.3 us
  local copies, waits for them, and re-layouts: 10.5 us -> 2.68 us
  other arithmetic: 2.95 us -> 9.67 us
    pallas_call x1, Pallas kernels: 92.8 us -> 84.3 us  [attention(): pl.pallas_call(functools.partial(attention_kernel, reach, lanes, tile, 1....]
    unnamed x7 -> x6, local copies, waits for them, and re-layouts: 9.78 us -> 1.95 us
    convert_element_type x0 -> x1, other arithmetic: none -> 6.73 us  [on_device(): return (dq.astype(jnp.float32), dk, dv)]
where the time goes in v2:
time: 98.2 us; the launch traced here: 97.3 us
  Pallas kernels  84.3 us (86%)
  other arithmetic  9.67 us (10%)
  local copies, waits for them, and re-layouts  2.68 us (3%)
    pallas_call x1, Pallas kernels, attention(): pl.pallas_call(functools.partial(attention_kernel, reach, lanes, tile, 1....  84.3 us
    convert_element_type x1, other arithmetic, on_device(): return (dq.astype(jnp.float32), dk, dv)  6.73 us

profile of v2, /device:TPU:1, one launch (start us, length us, event | category | flops | bytes accessed | tf_op | source)
XLA Modules:
  0.0 97.3 jit_solution(15796111996703058080)
XLA Ops:
  0.6 0.7 copy.12
  1.4 0.1 reduce
  1.5 0.7 sub.22
  2.2 0.1 select_reduce_fusion
  2.3 0.6 broadcast_subtract_fusion
  2.9 1.5 %multiply_bitcast_fusion.refs_5_ = f32[64,256]{1,0:T(8,128)} fusion(f32[256,64]{0,1:T(8,128)} %param.12), kind=kLoop, calls=%fused_computation | loop fusion | flops 16384 | bytes 131072 | tf_op jit(solution)/shard_map/transpose | solution.py:299
  4.3 84.3 %shard_map.94 = (bf16[256,8192]{1,0:T(8,128)(2,1)}, f32[256,1024]{1,0:T(8,128)}, f32[256,1024]{1,0:T(8,128)}) custom-call(bf16[256,8192]{1,0:T(8,128)(2,1)} %refs_0_.1, bf16[256,8192]{1,0:T(8,128)(2,1)} %refs_1_.1, bf16[256,8192]{1,0:T(8,128)(2,1)} %refs_2_.1, bf16[256,1024]{1,0:T(8,128)(2,1)} %refs_3_.1, bf16[256,1024]{1,0:T(8,128)(2,1)} %refs_4_.1, ...), custom_call_target="tpu_custom_call" | custom-call | tf_op jit(solution)/shard_map/pallas_call | solution.py:243
  88.6 0.0 copy-start.1
  88.6 0.0 copy-start
  88.6 6.7 %convert_element_type.3 = f32[256,8192]{1,0:T(8,128)} convert(bf16[256,8192]{1,0:T(8,128)(2,1)} %get-tuple-element.6) | non-fusion elementwise | flops 2097152 | bytes 12582912 | tf_op jit(solution)/shard_map/convert_element_type | solution.py:303
  95.4 0.0 copy-done.1
  95.4 1.0 copy.15
  96.3 0.0 copy-done
  96.3 1.0 copy.16
  (2 shorter events, 0.0 us)
Async XLA Ops:
  88.6 6.7 %copy-start.1 = (f32[256,1024]{1,0:T(8,128)S(1)}, f32[256,1024]{1,0:T(8,128)}, u32[]{:S(2)}) copy-start(f32[256,1024]{1,0:T(8,128)} %get-tuple-element.13) | copy-start | bytes 3145732
  88.6 7.7 %copy-start = (f32[256,1024]{1,0:T(8,128)S(1)}, f32[256,1024]{1,0:T(8,128)}, u32[]{:S(2)}) copy-start(f32[256,1024]{1,0:T(8,128)} %get-tuple-element.14) | copy-start | bytes 3145732
